TPU v7x, 32 devices: a whole 2x2x4 slice. The times are simulated.
32 devices in a mesh: dp: 2 (over core), ctx: 4 (over z), vocab: 4 (over y, x).
Axes of the slice: x: 2, y: 2, z: 4, core: 2. Of those that a mesh axis runs over, the one named last changes fastest.
Arguments:
- hidden: bfloat16 [512, 4096], P(('dp', 'ctx')), may hold values from -32 to 32
- head_weight: bfloat16 [4096, 9504], P(None, ('ctx', 'vocab')), may hold values from -2 to 2
- targets: int32 [512], P('dp'), may hold values from 0 to 9503
- segment_ids: int32 [512], P('dp'), may hold values from 0 to 31, as said below
- lengths: int32 [32], replicated, may hold values from 8 to 24, as said below
- loss_mask: int32 [512], P('dp'), may hold values 0 or 1
- advantages: float32 [32], replicated, may hold values from -4 to 4
- ref_logprobs: float32 [512], P('dp'), may hold values from -40 to -2
Outputs:
- grad_hidden: bfloat16 [512, 4096], P(('dp', 'ctx', 'vocab'))
- grad_head: bfloat16 [4096, 9504], P(None, ('ctx', 'vocab'))
Inputs may be any that keep to these rules, and one draw needn't show every extreme that they name: `segment_ids`: each sequence's tokens are contiguous; the tokens b * 64 to (b + 1) * 64 - 1 carry ids b * 4 to (b + 1) * 4 - 1, never falling, each id used. lengths[s] is the number of tokens whose segment id is s.
All inputs are finite; a program needn't handle non-finite values. No bound on the sum of `loss_mask` on one device may be relied on, other than what follows from the above.
Results may differ from a plain program's by a relative error of at most 0.012.
Values may be sent and summed in bfloat16 or wider, within the bound.
A program may use at most 128 MiB of HBM per device.

v0:
```python
import jax
import jax.numpy as jnp
from jax import lax
from jax.sharding import PartitionSpec as P

LOSS_SCALE = 1024
kl_weight = 0.1
entropy_weight = 0.05


def per_device(
    hidden, head_weight, targets, segment_ids, lengths, loss_mask, advantages, ref_logprobs
):
    vocab_width = head_weight.shape[1]
    first_column = (
        lax.axis_index("ctx") * lax.axis_size("vocab") + lax.axis_index("vocab")
    ) * vocab_width
    gathered = lax.all_gather(hidden, "ctx", axis=0, tiled=True)
    logits = jnp.dot(gathered, head_weight, preferred_element_type=jnp.float32)
    columns = first_column + lax.iota(jnp.int32, vocab_width)
    target_hits = targets[:, None] == columns[None, :]
    target_part = jnp.sum(jnp.where(target_hits, logits, 0.0), axis=1)
    row_max = lax.pmax(jnp.max(logits, axis=1), ("ctx", "vocab"))
    shifted = jnp.exp(logits - row_max[:, None])
    exp_total, exp_logit, target_logit = lax.psum(
        (jnp.sum(shifted, axis=1), jnp.sum(shifted * logits, axis=1), target_part), ("ctx", "vocab")
    )
    log_total = row_max + jnp.log(exp_total)
    target_logp = target_logit - log_total
    mean_logit = exp_logit / exp_total
    probs = jnp.exp(logits - log_total[:, None])
    seq_onehot = segment_ids[:, None] == lax.iota(jnp.int32, advantages.shape[0])[None, :]
    token_adv = jnp.sum(jnp.where(seq_onehot, advantages[None, :], 0.0), axis=1)
    token_len = jnp.sum(jnp.where(seq_onehot, lengths[None, :].astype(jnp.float32), 0.0), axis=1)
    token_weight = LOSS_SCALE * loss_mask.astype(jnp.float32) / token_len
    logp_grad = -token_adv + kl_weight * (target_logp - ref_logprobs)
    inner = logp_grad[:, None] * (target_hits.astype(jnp.float32) - probs)
    inner = inner + entropy_weight * probs * (logits - mean_logit[:, None])
    grad_logits = (token_weight[:, None] * inner).astype(jnp.bfloat16)
    head_local = lax.dot_general(
        gathered, grad_logits, (((0,), (0,)), ((), ())), preferred_element_type=jnp.float32
    ).astype(jnp.bfloat16)
    grad_head = lax.psum(head_local, "dp").astype(jnp.float32).astype(jnp.bfloat16)
    grad_hidden = lax.psum_scatter(
        lax.dot_general(
            grad_logits, head_weight, (((1,), (1,)), ((), ())), preferred_element_type=jnp.float32
        ),
        ("ctx", "vocab"),
        scatter_dimension=0,
        tiled=True,
    )
    return (grad_hidden.astype(jnp.bfloat16), grad_head)


def solution(mesh):
    return jax.shard_map(
        per_device,
        mesh=mesh,
        in_specs=(
            P(("dp", "ctx"), None),
            P(None, ("ctx", "vocab")),
            P("dp"),
            P("dp"),
            P(),
            P("dp"),
            P(),
            P("dp"),
        ),
        out_specs=(P(("dp", "ctx", "vocab"), None), P(None, ("ctx", "vocab"))),
        check_vma=False,
    )
```

profile of v0, /device:TPU:0, one launch (start us, length us, event | category | flops | bytes accessed | tf_op | source)
XLA Modules:
  0.0 282.1 jit_solution(3857916356808033694)
XLA Ops:
  7.2 0.0 all-gather.2.cloned.1.call-start
  7.2 0.7 all-gather.2.cloned.1.call-update
  7.9 0.0 reduce-scatter.2.cloned.1.call-start
  7.9 0.7 convert_element_type.25
  8.6 0.8 select_reduce_fusion.1
  9.4 0.7 multiply_divide_fusion
  10.1 0.0 copy-start.1
  10.1 0.0 copy-start.2
  10.1 47.9 %all-gather.2.cloned.1.call-done = bf16[256,4096]{1,0:T(8,128)(2,1)} async-done(((bf16[64,4096]{1,0:T(8,128)(2,1)}), bf16[256,4096]{1,0:T(8,128)(2,1)}) %all-gather.2.cloned.1.call-update) | async-done | bytes 2097168 | tf_op jit(solution)/shard_map/all_gather | solution.py:18
  58.0 4.5 %fusion.11 = (f32[256]{0:T(256)S(1)}, f32[256,594]{0,1:T(8,128)S(1)}) fusion(bf16[256,4096]{1,0:T(8,128)(2,1)} %all-gather.2.cloned.1.call-done, bf16[4096,594]{0,1:T(8,128)(2,1)} %param.9), kind=kOutput, calls=%fused_computation.21 | convolution fusion | flops 1245860096 | bytes 7572480 | tf_op jit(solution)/shard_map/dot_general | solution.py:19
  62.5 39.5 %pmax.7 = f32[256]{0:T(256)S(1)} all-reduce(f32[256]{0:T(256)S(1)} %get-tuple-element.13), channel_id=1, replica_groups=mesh['dp'=2,'ctx'=4,'vocab'=4] {'ctx','vocab'}, use_global_device_ids=true, to_apply=%region_5.6 | all-reduce | flops 256 | bytes 2048 | tf_op jit(solution)/shard_map/pmax | solution.py:23
  102.0 0.0 copy-done.1
  102.0 0.2 fusion.7
  102.2 36.6 %all-reduce = (f32[256]{0:T(256)S(1)}, f32[256]{0:T(256)S(1)}, f32[256]{0:T(256)S(1)}) all-reduce(f32[256]{0:T(256)S(1)} %get-tuple-element.3, f32[256]{0:T(256)S(1)} %get-tuple-element.2, f32[256]{0:T(256)S(1)} %get-tuple-element.4), channel_id=1, replica_groups=mesh['dp'=2,'ctx'=4,'vocab'=4] {'ctx','vocab'}, use_global_device_ids=true, to_apply=%region_9.10 | all-reduce | flops 768 | bytes 6144 | tf_op jit(solution)/shard_map/psum | solution.py:25
  138.8 0.0 copy-done.2
  138.8 6.5 %fusion.9 = f32[256,4096]{1,0:T(8,128)} fusion(bf16[4096,594]{0,1:T(8,128)(2,1)} %param.9, f32[256,594]{0,1:T(8,128)S(1)} %get-tuple-element.14, f32[256]{0:T(256)S(1)} %get-tuple-element.12, f32[256]{0:T(256)S(1)} %get-tuple-element.11, f32[256]{0:T(256)S(1)} %get-tuple-element.10, s32[256]{0:T(256)S(1)} %copy-done.1, f32[256]{0:T(256)S(1)} %multiply_divide_fusion, ...), kind=kOutput, calls=%fused_computation.20 | convolution fusion | flops 1247380992 | bytes 9676104 | tf_op jit(solution)/shard_map/dot_general | solution.py:45
  145.3 0.0 copy-start
  145.3 0.0 reduce-scatter.2.cloned.1.call-update
  145.3 0.0 all-reduce.3.cloned.1.call-start
  145.4 1.5 copy-done
  146.9 3.9 %fusion = bf16[4096,594]{0,1:T(8,128)(2,1)} fusion(bf16[256,4096]{1,0:T(8,128)(2,1)S(1)} %copy-done, f32[256,594]{0,1:T(8,128)S(1)} %get-tuple-element.14, f32[256]{0:T(256)S(1)} %get-tuple-element.12, f32[256]{0:T(256)S(1)} %get-tuple-element.11, f32[256]{0:T(256)S(1)} %get-tuple-element.10, s32[256]{0:T(256)S(1)} %copy-done.1, ...), kind=kOutput, calls=%fused_computation.1 | convolution fusion | flops 1249814016 | bytes 7578952 | tf_op jit(solution)/shard_map/dot_general | solution.py:40
  150.7 0.0 all-reduce.3.cloned.1.call-update
  150.8 87.7 %reduce-scatter.2.cloned.1.call-done = f32[16,4096]{1,0:T(8,128)} async-done(((f32[256,4096]{1,0:T(8,128)}), f32[16,4096]{1,0:T(8,128)}) %reduce-scatter.2.cloned.1.call-update) | async-done | bytes 262160 | tf_op jit(solution)/shard_map/reduce_scatter | solution.py:44
  238.5 1.6 convert_element_type.28
  240.1 30.2 %all-reduce.3.cloned.1.call-done = bf16[4096,594]{0,1:T(8,128)(2,1)} async-done(((bf16[4096,594]{0,1:T(8,128)(2,1)}), bf16[4096,594]{0,1:T(8,128)(2,1)}) %all-reduce.3.cloned.1.call-update) | async-done | bytes 4866064 | tf_op jit(solution)/shard_map/psum | solution.py:43
  270.3 5.2 %copy.11 = bf16[4096,594]{0,1:T(8,128)(2,1)} copy(bf16[4096,594]{0,1:T(8,128)(2,1)} %all-reduce.3.cloned.1.call-done) | data formatting | bytes 9732096
  (2 shorter events, 0.0 us)
Async XLA Ops:
  7.2 50.8 %all-gather.2.cloned.1.call-start = ((), (), s32[]{:S(2)}) async-start(), calls=%async_computation.1 | async-start | bytes 2621440 | tf_op jit(solution)/shard_map/all_gather | solution.py:18
  7.9 230.6 %reduce-scatter.2.cloned.1.call-start = ((), (), s32[]{:S(2)}) async-start(), calls=%async_computation.2 | async-start | bytes 4456448 | tf_op jit(solution)/shard_map/reduce_scatter | solution.py:44
  10.1 91.9 %copy-start.1 = (s32[256]{0:T(256)S(1)}, s32[256]{0:T(256)}, u32[]{:S(2)}) copy-start(s32[256]{0:T(256)} %param.10) | copy-start | bytes 3076
  10.1 128.7 %copy-start.2 = (f32[256]{0:T(256)S(1)}, f32[256]{0:T(256)}, u32[]{:S(2)}) copy-start(f32[256]{0:T(256)} %param.15) | copy-start | bytes 3076
  145.3 1.6 copy-start
  145.3 125.0 %all-reduce.3.cloned.1.call-start = ((), (), s32[]{:S(2)}) async-start(), calls=%async_computation.3 | async-start | bytes 9830400 | tf_op jit(solution)/shard_map/psum | solution.py:43
Sparse Core Ops, SparseCore 0:
  9.5 48.3 all-gather.1
  145.4 93.0 reduce-scatter.1
  241.6 28.6 all-reduce.2
where the time goes:
time: 282 us
  waiting for transfers between devices  167 us (59%)
  blocking collectives  76.1 us (27%)
  matrix products  14.9 us (5%)
  between operations  13.8 us (5%)
  local copies, waits for them, and re-layouts  6.77 us (2%)
  other arithmetic  3.95 us (1%)
    reduce_scatter x1, waiting for transfers between devices, per_device(): lax.psum_scatter(lax.dot_general(grad_logits, head_weight, (((1,), (1,)),...  87.7 us
    all_gather x1, waiting for transfers between devices, per_device(): gathered = lax.all_gather(hidden, 'ctx', axis=0, tiled=True)  47.9 us
    pmax x1, blocking collectives, per_device(): row_max = lax.pmax(jnp.max(logits, axis=1), ('ctx', 'vocab'))  39.5 us
    psum x1, blocking collectives, per_device(): lax.psum((jnp.sum(shifted, axis=1), jnp.sum(shifted * logits, axis=1), ta...  36.6 us
    psum x1, waiting for transfers between devices, per_device(): lax.psum(head_local, 'dp').astype(jnp.float32).astype(jnp.bfloat16)  30.2 us
    unnamed x7, local copies, waits for them, and re-layouts  6.77 us
    dot_general x1, matrix products, per_device(): lax.dot_general(grad_logits, head_weight, (((1,), (1,)), ((), ())), prefe...  6.48 us
  transfers between devices with their start and end apart: 3, of which 3 were waited for; matrix products, arithmetic and copies ran while one was open for 3% of the time, Pallas kernels for 0%

commit v1 on v0

--- a/solution.py
+++ b/solution.py
@@ -15,7 +15,12 @@
     first_column = (
         lax.axis_index("ctx") * lax.axis_size("vocab") + lax.axis_index("vocab")
     ) * vocab_width
-    gathered = lax.all_gather(hidden, "ctx", axis=0, tiled=True)
+    ring = [hidden]
+    for hop in range(3):
+        ring.append(lax.ppermute(ring[-1], "ctx", [(dev, (dev + 1) % 4) for dev in range(4)]))
+    gathered = jnp.roll(
+        jnp.concatenate(ring[::-1], axis=0), (lax.axis_index("ctx") + 1) * ring[0].shape[0], axis=0
+    )
     logits = jnp.dot(gathered, head_weight, preferred_element_type=jnp.float32)
     columns = first_column + lax.iota(jnp.int32, vocab_width)
     target_hits = targets[:, None] == columns[None, :]

time: 282 us -> 246 us (0.87)
  waiting for transfers between devices: 167 us -> 128 us
  starting transfers between devices: 0.12 us -> 3.19 us
    all_gather x1 -> x0, waiting for transfers between devices: 47.9 us -> none  [per_device(): gathered = lax.all_gather(hidden, 'ctx', axis=0, tiled=True)]
    ppermute x0 -> x3, waiting for transfers between devices: none -> 41 us  [per_device(): lax.ppermute(ring[-1], 'ctx', [(dev, (dev + 1) % 4) for dev in range(4)])]
    psum x1, waiting for transfers between devices: 30.2 us -> 0.01 us  [per_device(): lax.psum(head_local, 'dp').astype(jnp.float32).astype(jnp.bfloat16)]
    ppermute x0 -> x3, starting transfers between devices: none -> 3.11 us  [per_device(): lax.ppermute(ring[-1], 'ctx', [(dev, (dev + 1) % 4) for dev in range(4)])]
    dot_general x1, matrix products: 4.53 us -> 1.63 us  [per_device(): logits = jnp.dot(gathered, head_weight, preferred_element_type=jnp.float32)]
    unnamed x7 -> x18, local copies, waits for them, and re-layouts: 6.77 us -> 6.82 us
  transfers between devices with their start and end apart: 3 -> 5, of which waited for: 3 -> 4; matrix products, arithmetic and copies ran while one was open for 3% -> 4% of each run, Pallas kernels for 0% -> 0%
where the time goes in v1:
time: 246 us
  waiting for transfers between devices  128 us (52%)
  blocking collectives  75.2 us (31%)
  between operations  15.6 us (6%)
  matrix products  13.5 us (5%)
  local copies, waits for them, and re-layouts  6.86 us (3%)
  other arithmetic  3.95 us (2%)
  starting transfers between devices  3.19 us (1%)
    reduce_scatter x1, waiting for transfers between devices, per_device(): lax.psum_scatter(lax.dot_general(grad_logits, head_weight, (((1,), (1,)),...  86.7 us
    ppermute x3, waiting for transfers between devices, per_device(): lax.ppermute(ring[-1], 'ctx', [(dev, (dev + 1) % 4) for dev in range(4)])  41 us
    pmax x1, blocking collectives, per_device(): row_max = lax.pmax(jnp.max(logits, axis=1), ('ctx', 'vocab'))  37.6 us
    psum x1, blocking collectives, per_device(): lax.psum((jnp.sum(shifted, axis=1), jnp.sum(shifted * logits, axis=1), ta...  37.5 us
    unnamed x18, local copies, waits for them, and re-layouts  6.82 us
    dot_general x1, matrix products, per_device(): lax.dot_general(grad_logits, head_weight, (((1,), (1,)), ((), ())), prefe...  6.47 us
    dot_general x1, matrix products, per_device(): lax.dot_general(gathered, grad_logits, (((0,), (0,)), ((), ())), preferre...  5.41 us
  transfers between devices with their start and end apart: 5, of which 4 were waited for; matrix products, arithmetic and copies ran while one was open for 4% of the time, Pallas kernels for 0%

profile of v1, /device:TPU:0, one launch (start us, length us, event | category | flops | bytes accessed | tf_op | source)
XLA Modules:
  0.0 246.0 jit_solution(9360287773270463425)
XLA Ops:
  8.0 0.0 copy-start.1
  8.0 0.0 reduce-scatter.2.cloned.1.call-start
  8.1 3.1 %collective-permute-start = (bf16[64,4096]{1,0:T(8,128)(2,1)}, bf16[64,4096]{1,0:T(8,128)(2,1)S(1)}, u32[]{:S(2)}, u32[]{:S(2)}) collective-permute-start(bf16[64,4096]{1,0:T(8,128)(2,1)} %param.8), channel_id=1, source_target_pairs={{0,4},{4,8},{8,12},{12,0},{1,5},{5,9},{9,13},{13,1},{2,6},{6,10},{... | collective-permute-start | bytes 1572872 | tf_op jit(solution)/shard_map/ppermute | solution.py:20
  11.2 14.2 %collective-permute-done = bf16[64,4096]{1,0:T(8,128)(2,1)S(1)} collective-permute-done((bf16[64,4096]{1,0:T(8,128)(2,1)}, bf16[64,4096]{1,0:T(8,128)(2,1)S(1)}, u32[]{:S(2)}, u32[]{:S(2)}) %collective-permute-start) | collective-permute-done | bytes 524320 | tf_op jit(solution)/shard_map/ppermute | solution.py:20
  25.3 0.0 collective-permute-start.1
  25.3 14.9 %collective-permute-done.1 = bf16[64,4096]{1,0:T(8,128)(2,1)S(1)} collective-permute-done((bf16[64,4096]{1,0:T(8,128)(2,1)S(1)}, bf16[64,4096]{1,0:T(8,128)(2,1)S(1)}, u32[]{:S(2)}, u32[]{:S(2)}) %collective-permute-start.1) | collective-permute-done | bytes 524320 | tf_op jit(solution)/shard_map/ppermute | solution.py:20
  40.2 0.0 collective-permute-start.2
  40.2 0.7 convert_element_type.22
  40.9 0.8 select_reduce_fusion.1
  41.6 0.7 multiply_divide_fusion
  42.3 0.0 copy-start
  42.3 11.9 %collective-permute-done.2 = bf16[64,4096]{1,0:T(8,128)(2,1)S(1)} collective-permute-done((bf16[64,4096]{1,0:T(8,128)(2,1)S(1)}, bf16[64,4096]{1,0:T(8,128)(2,1)S(1)}, u32[]{:S(2)}, u32[]{:S(2)}) %collective-permute-start.2) | collective-permute-done | bytes 524320 | tf_op jit(solution)/shard_map/ppermute | solution.py:20
  54.4 1.1 constant_dynamic-update-slice_fusion.4
  55.6 0.0 copy-done.1
  55.6 0.0 copy-done
  55.6 0.0 copy-start.2
  55.7 0.0 copy-start.3
  55.7 0.0 copy-start.4
  55.7 1.6 fusion.15
  57.3 0.3 copy-done.2
  57.6 37.6 %pmax.7 = f32[256]{0:T(256)S(1)} all-reduce(f32[256]{0:T(256)S(1)} %get-tuple-element.13), channel_id=1, replica_groups=mesh['dp'=2,'ctx'=4,'vocab'=4] {'ctx','vocab'}, use_global_device_ids=true, to_apply=%region_5.6 | all-reduce | flops 256 | bytes 2048 | tf_op jit(solution)/shard_map/pmax | solution.py:28
  95.2 0.0 copy-done.3
  95.2 0.2 fusion.9
  95.4 37.5 %all-reduce = (f32[256]{0:T(256)S(1)}, f32[256]{0:T(256)S(1)}, f32[256]{0:T(256)S(1)}) all-reduce(f32[256]{0:T(256)S(1)} %get-tuple-element.3, f32[256]{0:T(256)S(1)} %get-tuple-element.2, f32[256]{0:T(256)S(1)} %get-tuple-element.4), channel_id=1, replica_groups=mesh['dp'=2,'ctx'=4,'vocab'=4] {'ctx','vocab'}, use_global_device_ids=true, to_apply=%region_9.10 | all-reduce | flops 768 | bytes 6144 | tf_op jit(solution)/shard_map/psum | solution.py:30
  132.9 0.0 copy-done.4
  133.0 6.5 %fusion.13 = f32[256,4096]{1,0:T(8,128)} fusion(bf16[4096,594]{0,1:T(8,128)(2,1)} %param.9, f32[256,594]{0,1:T(8,128)S(1)} %get-tuple-element.14, f32[256]{0:T(256)S(1)} %get-tuple-element.12, f32[256]{0:T(256)S(1)} %get-tuple-element.11, f32[256]{0:T(256)S(1)} %get-tuple-element.10, s32[256]{0:T(256)S(1)} %copy-done.3, f32[256]{0:T(256)S(1)} %multiply_divide_fusion, ...), kind=kOutput, calls=%fused_computation.32 | convolution fusion | flops 1247380992 | bytes 9676104 | tf_op jit(solution)/shard_map/dot_general | solution.py:50
  139.4 0.0 reduce-scatter.2.cloned.1.call-update
  139.5 0.0 all-reduce.3.cloned.1.call-start
  139.5 5.4 %convolution_convert_fusion = bf16[4096,594]{0,1:T(8,128)(2,1)} fusion(bf16[512,4096]{1,0:T(8,128)(2,1)} %copy-done.2, s32[]{:T(128)S(6)} %select_n.27, f32[256,594]{0,1:T(8,128)S(1)} %get-tuple-element.14, f32[256]{0:T(256)S(1)} %get-tuple-element.12, f32[256]{0:T(256)S(1)} %get-tuple-element.11, f32[256]{0:T(256)S(1)} %get-tuple-element.10, ...), kind=kOutput, calls=%fused_computation | convolution fusion | flops 1249814016 | bytes 7578956 | tf_op jit(solution)/shard_map/dot_general | solution.py:45
  144.9 0.0 all-reduce.3.cloned.1.call-update
  144.9 86.7 %reduce-scatter.2.cloned.1.call-done = f32[16,4096]{1,0:T(8,128)} async-done(((f32[256,4096]{1,0:T(8,128)}), f32[16,4096]{1,0:T(8,128)}) %reduce-scatter.2.cloned.1.call-update) | async-done | bytes 262160 | tf_op jit(solution)/shard_map/reduce_scatter | solution.py:49
  231.6 1.6 convert_element_type.25
  233.3 0.0 all-reduce.3.cloned.1.call-done
  233.3 5.2 %copy.18 = bf16[4096,594]{0,1:T(8,128)(2,1)} copy(bf16[4096,594]{0,1:T(8,128)(2,1)} %all-reduce.3.cloned.1.call-done) | data formatting | bytes 9732096
  (9 shorter events, 0.3 us)
Async XLA Ops:
  8.0 47.6 %copy-start.1 = (bf16[64,4096]{1,0:T(8,128)(2,1)S(1)}, bf16[64,4096]{1,0:T(8,128)(2,1)}, u32[]{:S(2)}) copy-start(bf16[64,4096]{1,0:T(8,128)(2,1)} %param.8) | copy-start | bytes 1572868
  8.0 223.6 %reduce-scatter.2.cloned.1.call-start = ((), (), s32[]{:S(2)}) async-start(), calls=%async_computation.1 | async-start | bytes 4456448 | tf_op jit(solution)/shard_map/reduce_scatter | solution.py:49
  8.1 17.3 %collective-permute-start = (bf16[64,4096]{1,0:T(8,128)(2,1)}, bf16[64,4096]{1,0:T(8,128)(2,1)S(1)}, u32[]{:S(2)}, u32[]{:S(2)}) collective-permute-start(bf16[64,4096]{1,0:T(8,128)(2,1)} %param.8), channel_id=1, source_target_pairs={{0,4},{4,8},{8,12},{12,0},{1,5},{5,9},{9,13},{13,1},{2,6},{6,10},{... | collective-permute-start | bytes 1572872 | tf_op jit(solution)/shard_map/ppermute | solution.py:20
  25.3 14.9 %collective-permute-start.1 = (bf16[64,4096]{1,0:T(8,128)(2,1)S(1)}, bf16[64,4096]{1,0:T(8,128)(2,1)S(1)}, u32[]{:S(2)}, u32[]{:S(2)}) collective-permute-start(bf16[64,4096]{1,0:T(8,128)(2,1)S(1)} %collective-permute-done), channel_id=1, source_target_pairs={{0,4},{4,8},{8,12},{12,0},{1,5},{5,9},{9,13},{13,1},{2,6},{6,10},{... | collective-permute-start | bytes 1572872 | tf_op jit(solution)/shard_map/ppermute | solution.py:20
  40.2 14.0 %collective-permute-start.2 = (bf16[64,4096]{1,0:T(8,128)(2,1)S(1)}, bf16[64,4096]{1,0:T(8,128)(2,1)S(1)}, u32[]{:S(2)}, u32[]{:S(2)}) collective-permute-start(bf16[64,4096]{1,0:T(8,128)(2,1)S(1)} %collective-permute-done.1), channel_id=1, source_target_pairs={{0,4},{4,8},{8,12},{12,0},{1,5},{5,9},{9,13},{13,1},{2,6},{6,10},{... | collective-permute-start | bytes 1572872 | tf_op jit(solution)/shard_map/ppermute | solution.py:20
  42.3 13.3 %copy-start = (bf16[4096,594]{0,1:T(8,128)(2,1)S(1)}, bf16[4096,594]{0,1:T(8,128)(2,1)}, u32[]{:S(2)}) copy-start(bf16[4096,594]{0,1:T(8,128)(2,1)} %param.9) | copy-start | bytes 14598148
  55.6 1.9 copy-start.2
  55.7 39.6 %copy-start.3 = (s32[256]{0:T(256)S(1)}, s32[256]{0:T(256)}, u32[]{:S(2)}) copy-start(s32[256]{0:T(256)} %param.10) | copy-start | bytes 3076
  55.7 77.3 %copy-start.4 = (f32[256]{0:T(256)S(1)}, f32[256]{0:T(256)}, u32[]{:S(2)}) copy-start(f32[256]{0:T(256)} %param.15) | copy-start | bytes 3076
  139.5 93.8 %all-reduce.3.cloned.1.call-start = ((), (), s32[]{:S(2)}) async-start(), calls=%async_computation.2 | async-start | bytes 9830400 | tf_op jit(solution)/shard_map/psum | solution.py:48
Sparse Core Ops, SparseCore 0:
  139.6 92.0 reduce-scatter.1
Sparse Core Ops, SparseCore 1:
  145.0 25.4 all-reduce.2
